TPU v7x, 32 devices: a whole 2x2x4 slice. The times are simulated.
32 devices in a mesh: req: 8 (over y, x, core), tp: 4 (over z).
Axes of the slice: x: 2, y: 2, z: 4, core: 2. Of those that a mesh axis runs over, the one named last changes fastest.
Arguments:
- new_query: bfloat16 [1024, 2560], P('req', 'tp'), may hold values from -64 to 64
- new_keyval: bfloat16 [1024, 1280], P('req', 'tp'), may hold values from -24 to 24
- residual_in: bfloat16 [1024, 2560], P('req'), may hold values from -64 to 64
- leaf_cache: bfloat16 [128, 32, 1280], P('req', None, 'tp'), may hold values from -6 to 6
- leaf_length: int32 [128], P('req'), may hold values from 1 to 32
- new_counts: int32 [8, 16], P('req'), may hold values from 1 to 16, as said below
- request_mid: int32 [128], P('req'), may hold values from 0 to 5
- mid_root: int32 [6], replicated, may hold values from 0 to 1, as said below
- node_length: int32 [8], replicated, may hold values from 1 to 1744, as said below
- prefix_pool: bfloat16 [256, 16, 1280], P('req', None, 'tp'), may hold values from -6 to 6
- page_node: int32 [256], P('req'), may hold values from -1 to 7, as said below
- page_rank: int32 [256], P('req'), may hold values from 0 to 108, as said below
- out_weight: bfloat16 [2560, 2560], P('tp'), may hold values from -0.125 to 0.125
- norm_gain: bfloat16 [2560], replicated, may hold values from 0.5 to 1.5
- gate_weight: bfloat16 [2560, 3584], P(None, 'tp'), may hold values from -0.125 to 0.125
- up_weight: bfloat16 [2560, 3584], P(None, 'tp'), may hold values from -0.125 to 0.125
- down_weight: bfloat16 [3584, 2560], P('tp'), may hold values from -0.09375 to 0.09375
- next_gain: bfloat16 [2560], replicated, may hold values from 0.5 to 1.5
- query_weight: bfloat16 [2560, 2560], P(None, 'tp'), may hold values from -0.125 to 0.125
- keyval_weight: bfloat16 [2560, 1280], P(None, 'tp'), may hold values from -0.125 to 0.125
Outputs:
- attention: bfloat16 [1024, 2560], P('req', 'tp')
- residual_out: bfloat16 [1024, 2560], P(('req', 'tp'))
- next_query: bfloat16 [1024, 2560], P('req', 'tp')
- next_keyval: bfloat16 [1024, 1280], P('req', 'tp')
Inputs may be any that keep to these rules, and one draw needn't show every extreme that they name: `new_counts`: each row sums to 128 and holds one request of exactly 16 new tokens. `mid_root`: each root is the parent of 3 mid-level nodes. `node_length`: A node of k pages has more than 16 * (k - 1) and at most 16 * k prefix tokens; a node with the most pages has exactly 16 * k. `page_node`: every node owns one page or more; 32 pages are free (-1). `page_rank`: the k pages of a node carry the ranks 0 to k - 1, each once; free pages carry 0.
All inputs are finite; a program needn't handle non-finite values.
Results may differ from a plain program's by a relative error of at most 0.015.
Values may be sent and summed in bfloat16 or wider, within the bound.
No kernel may reach another device: no remote copies, remote signals or barrier semaphores. Data moves between devices by JAX's collectives and lax.ppermute only.
A program may use at most 128 MiB of HBM per device.

v0:
```python
import math
import jax
import jax.numpy as jnp
from jax import lax
from jax.sharding import PartitionSpec as P

HD = 80
MAXNEW = 16
ROOTS = 2
MIDS = 6
NODES = 8
MASKED = -1e30
EPSILON = 1e-05


def rms_scale(values_in, gain):
    values = values_in.astype(jnp.float32)
    scale = lax.rsqrt(jnp.mean(values * values, axis=-1, keepdims=True) + EPSILON)
    return (values * scale * gain.astype(jnp.float32)).astype(jnp.bfloat16)


def combine(first, second):
    top_first, total_first, sum_first = first
    top_second, total_second, sum_second = second
    top = jnp.maximum(top_first, top_second)
    factor_first = jnp.exp(top_first - top)
    factor_second = jnp.exp(top_second - top)
    total = total_first * factor_first + total_second * factor_second
    weighted = sum_first * factor_first[..., None] + sum_second * factor_second[..., None]
    return (top, total, weighted)


def attend(queries, keys, values, visible):
    scores = jnp.einsum("nkgd,mkd->nkgm", queries, keys, preferred_element_type=jnp.float32) * (
        1.0 / math.sqrt(HD)
    )
    shown = visible[:, None, None, :]
    scores = jnp.where(shown, scores, MASKED)
    top = jnp.max(scores, axis=-1)
    raised = jnp.where(shown, jnp.exp(scores - top[..., None]), 0.0)
    total = jnp.sum(raised, axis=-1)
    weighted = jnp.einsum(
        "nkgm,mkd->nkgd", raised.astype(jnp.bfloat16), values, preferred_element_type=jnp.float32
    )
    return (top, total, weighted)


def pool_split(pages_in, node_of_page, rank_of_page):
    page_count = pages_in.shape[0]
    page_size = pages_in.shape[1]
    flat = pages_in.reshape(page_count * page_size, pages_in.shape[2] // (2 * HD), 2, HD)
    key_node = jnp.repeat(node_of_page, page_size, total_repeat_length=page_count * page_size)
    key_place = (
        rank_of_page[:, None] * page_size + jnp.arange(page_size, dtype=jnp.int32)[None, :]
    ).reshape(page_count * page_size)
    return (flat[:, :, 0], flat[:, :, 1], key_node, key_place)


def shared_visible(token_info, key_node, key_place):
    root_hit = (key_node[None, :] == token_info[:, 0:1]) & (key_place[None, :] < token_info[:, 2:3])
    mid_hit = (key_node[None, :] == token_info[:, 1:2]) & (key_place[None, :] < token_info[:, 3:4])
    return root_hit | mid_hit


def token_tables(counts, request_mid, mid_root, node_length, row_count):
    requests = counts.shape[0]
    starts = jnp.cumsum(counts) - counts
    index = jnp.arange(row_count, dtype=jnp.int32)
    owner = jnp.sum((index[:, None] >= starts[None, :]).astype(jnp.int32), axis=1) - 1
    pick = (owner[:, None] == jnp.arange(requests, dtype=jnp.int32)[None, :]).astype(jnp.int32)
    offset = index - jnp.sum(pick * starts[None, :], axis=1)
    token_mid = jnp.sum(pick * request_mid[None, :], axis=1)
    mid_pick = (token_mid[:, None] == jnp.arange(MIDS, dtype=jnp.int32)[None, :]).astype(jnp.int32)
    token_root = jnp.sum(mid_pick * mid_root[None, :], axis=1)
    mid_node = token_mid + ROOTS
    node_ids = jnp.arange(NODES, dtype=jnp.int32)
    root_len = jnp.sum(
        (token_root[:, None] == node_ids[None, :]).astype(jnp.int32) * node_length[None, :], axis=1
    )
    mid_len = jnp.sum(
        (mid_node[:, None] == node_ids[None, :]).astype(jnp.int32) * node_length[None, :], axis=1
    )
    token_info = jnp.stack([token_root, mid_node, root_len, mid_len], axis=1)
    return (starts, owner, offset, token_info)


def local_part(
    new_query, new_keyval, leaf_cache, leaf_length, counts, starts, owner, offset, kv_local, group
):
    requests = counts.shape[0]
    leaf_slots = leaf_cache.shape[1]
    slot = jnp.arange(MAXNEW, dtype=jnp.int32)
    row_index = jnp.clip(starts[:, None] + slot[None, :], 0, new_query.shape[0] - 1)
    pad_query = new_query[row_index].reshape(requests, MAXNEW, kv_local, group, HD)
    pad_keyval = new_keyval[row_index]
    joined = jnp.concatenate([leaf_cache, pad_keyval], axis=1).reshape(
        requests, leaf_slots + MAXNEW, kv_local, 2, HD
    )
    leaf_ok = jnp.broadcast_to(
        jnp.arange(leaf_slots, dtype=jnp.int32)[None, None, :] < leaf_length[:, None, None],
        (requests, MAXNEW, leaf_slots),
    )
    causal = jnp.broadcast_to(
        slot[None, None, :] <= slot[None, :, None], (requests, MAXNEW, MAXNEW)
    )
    visible = jnp.concatenate([leaf_ok, causal], axis=2)
    part = jax.vmap(attend)(pad_query, joined[:, :, :, 0], joined[:, :, :, 1], visible)
    flat = owner * MAXNEW + offset
    return tuple((item.reshape((requests * MAXNEW,) + item.shape[2:])[flat] for item in part))


def visit_owners(new_query, token_info, prefix_pool, page_node, page_rank, kv_local, group):
    all_query, all_info = (
        lax.all_gather(new_query, "req", axis=0, tiled=True),
        lax.all_gather(token_info, "req", axis=0, tiled=True),
    )
    total_rows = all_query.shape[0]
    block = math.gcd(total_rows, 512)
    keys, values, key_node, key_place = pool_split(prefix_pool, page_node, page_rank)

    def owner_block(items):
        query_block, info_block = items
        heads = query_block.reshape(block, kv_local, group, HD)
        return attend(heads, keys, values, shared_visible(info_block, key_node, key_place))

    part = lax.map(
        owner_block,
        (
            all_query.reshape(total_rows // block, block, all_query.shape[1]),
            all_info.reshape(total_rows // block, block, 4),
        ),
    )
    holders = lax.axis_size("req")
    row_count = total_rows // holders
    part_top, part_total, part_sum = tuple(
        (item.reshape((holders, row_count) + item.shape[2:]) for item in part)
    )
    tops, totals, sums = (
        lax.all_to_all(part_top, "req", split_axis=0, concat_axis=0, tiled=True),
        lax.all_to_all(part_total, "req", split_axis=0, concat_axis=0, tiled=True),
        lax.all_to_all(part_sum, "req", split_axis=0, concat_axis=0, tiled=True),
    )
    top = jnp.max(tops, axis=0)
    factor = jnp.exp(tops - top[None])
    return (top, jnp.sum(totals * factor, axis=0), jnp.sum(sums * factor[..., None], axis=0))


def per_device(
    new_query,
    new_keyval,
    residual_in,
    leaf_cache,
    leaf_length,
    new_counts,
    request_mid,
    mid_root,
    node_length,
    prefix_pool,
    page_node,
    page_rank,
    out_weight,
    norm_gain,
    gate_weight,
    up_weight,
    down_weight,
    next_gain,
    query_weight,
    keyval_weight,
):
    row_count = new_query.shape[0]
    query_width = new_query.shape[1]
    keyval_width = new_keyval.shape[1]
    kv_local = keyval_width // (2 * HD)
    group = query_width // (kv_local * HD)
    counts = new_counts[0]
    starts, owner, offset, token_info = token_tables(
        counts, request_mid, mid_root, node_length, row_count
    )
    shared = visit_owners(new_query, token_info, prefix_pool, page_node, page_rank, kv_local, group)
    local = local_part(
        new_query,
        new_keyval,
        leaf_cache,
        leaf_length,
        counts,
        starts,
        owner,
        offset,
        kv_local,
        group,
    )
    top, total, weighted = combine(shared, local)
    attention = (weighted / total[..., None]).reshape(row_count, query_width).astype(jnp.bfloat16)
    share = row_count // lax.axis_size("tp")
    mine = lax.axis_index("tp") * share
    attn_proj = lax.psum(jnp.dot(attention, out_weight, preferred_element_type=jnp.float32), "tp")
    mixed = (residual_in.astype(jnp.float32) + attn_proj).astype(jnp.bfloat16)
    normed = rms_scale(mixed, norm_gain)
    gate = jnp.dot(normed, gate_weight, preferred_element_type=jnp.float32)
    upward = jnp.dot(normed, up_weight, preferred_element_type=jnp.float32)
    hidden = (jax.nn.silu(gate) * upward).astype(jnp.bfloat16)
    mlp_proj = lax.psum(jnp.dot(hidden, down_weight, preferred_element_type=jnp.float32), "tp")
    layer_rows = (mixed.astype(jnp.float32) + mlp_proj).astype(jnp.bfloat16)
    residual_out = lax.dynamic_slice_in_dim(layer_rows, mine, share, 0)
    final = rms_scale(layer_rows, next_gain)
    next_query = jnp.dot(final, query_weight, preferred_element_type=jnp.float32).astype(
        jnp.bfloat16
    )
    next_keyval = jnp.dot(final, keyval_weight, preferred_element_type=jnp.float32).astype(
        jnp.bfloat16
    )
    return (attention, residual_out, next_query, next_keyval)


def solution(mesh):
    in_specs = (
        P("req", "tp"),
        P("req", "tp"),
        P("req", None),
        P("req", None, "tp"),
        P("req"),
        P("req", None),
        P("req"),
        P(),
        P(),
        P("req", None, "tp"),
        P("req"),
        P("req"),
        P("tp", None),
        P(),
        P(None, "tp"),
        P(None, "tp"),
        P("tp", None),
        P(),
        P(None, "tp"),
        P(None, "tp"),
    )
    out_specs = (P("req", "tp"), P(("req", "tp"), None), P("req", "tp"), P("req", "tp"))
    return jax.shard_map(
        per_device, mesh=mesh, in_specs=in_specs, out_specs=out_specs, check_vma=False
    )
```

profile of v0, /device:TPU:0, one launch (start us, length us, event | category | flops | bytes accessed | tf_op | source)
XLA Modules:
  0.0 375.2 jit_solution(16658785647169500201)
XLA Ops:
  8.0 0.9 copy.127
  10.4 2.1 reshape.441
  12.5 3.1 fusion.62
  16.4 1.8 copy.129
  18.2 1.8 copy.128
  20.8 11.4 %all_gather.6 = s32[1024,4]{0,1:T(4,128)} all-gather(s32[128,4]{0,1:T(4,128)S(1)} %pad_add_fusion.1), channel_id=1, replica_groups=mesh['req'=8,'tp'=4] {'req'}, dimensions={0}, use_global_device_ids=true | all-gather | bytes 18432 | tf_op jit(solution)/shard_map/all_gather | solution.py:115
  33.8 4.2 %compare_select_fusion.2 = (s32[512,1]{0,1:T(1,128)S(1)}, s32[512,1]{0,1:T(1,128)S(1)}) fusion(s32[]{:T(128)} %bitcast.29, s32[]{:T(128)} %bitcast.30, s32[]{:T(128)} %bitcast.31, s32[]{:T(128)} %bitcast.32, s32[]{:T(128)} %bitcast.33, s32[]{:T(128)} %bitcast.35, s32[]{:T(128)} %bitcast.34, s32[512,1]{0,1:T(1,128)S(1)} %bitcast.213, s32[512,1]{0,1:T(1,128)S(1)} %bitcast.212), kind=kLoop, calls=%fused_computation.105 | loop fusion | flops 7168 | bytes 8220 | tf_op jit(solution)/shard_map/jit(_take)/gather | solution.py:52
  38.6 16.0 %select_select_fusion = s32[512]{0:T(512)} fusion(pred[512]{0:T(512)(128)(4,1)S(1)} %get-tuple-element.200, pred[512]{0:T(512)(128)(4,1)S(1)} %get-tuple-element.199, pred[512]{0:T(512)(128)(4,1)S(1)} %get-tuple-element.198, pred[512]{0:T(512)(128)(4,1)S(1)} %get-tuple-element.197, pred[512]{0:T(512)(128)(4,1)S(1)} %get-tuple-element.196, ...), kind=kLoop, calls=%fused_computation.129 | loop fusion | flops 17408 | bytes 19060 | tf_op jit(solution)/shard_map/jit(_take)/select_n | solution.py:52
  54.6 100.4 %while.16 = (s32[]{:T(128)}, f32[2,512,2,4]{1,0,3,2:T(2,128)}, f32[2,512,2,4]{1,0,3,2:T(2,128)}, f32[2,512,2,4,80]{1,0,4,3,2:T(2,128)}, s32[512]{0:T(512)}, /*in...) while((s32[]{:T(128)}, f32[2,512,2,4]{1,0,3,2:T(2,128)}, ...), condition=%wide.region_9.10_spmd.clone, body=%wide.region_6.0_spmd.clone.sunk | while | flops 700178944 | bytes 71092600 | solution.py:126
  56.7 1.2 and_or_fusion.2
  57.8 2.0 constant_dynamic-slice_fusion.3
  59.8 2.2 copy.193
  62.0 5.8 %bitcast_reduce_fusion.2 = (f32[512,2,4]{0,2,1:T(4,128)S(1)}, f32[2,512,4,512]{1,3,2,0:T(8,128)}) fusion(pred[512,512]{0,1:T(8,128)(4,1)S(1)} %and_or_fusion.2, bf16[512,2,4,80]{0,3,2,1:T(8,128)(2,1)} %bitcast.188, bf16[512,2,80]{0,2,1:T(8,128)(2,1)} %get-tuple-element.391), kind=kOutput, calls=%fused_computation.7.clone.1 | convolution fusion | flops 341831680 | bytes 9486336 | tf_op jit(solution)/shard_map/while/body/eval_jaxpr/nkgd,mkd->nkgm/dot_general | solution.py:34
  68.5 1.4 dynamic_update_slice.17
  69.9 4.6 %fusion.85 = f32[512,2,4]{0,2,1:T(4,128)S(1)} fusion(f32[2,512,4,512]{1,3,2,0:T(8,128)} %get-tuple-element.359, f32[512,2,4]{0,2,1:T(4,128)S(1)} %get-tuple-element.358, pred[512,512]{0,1:T(8,128)(4,1)S(1)} %and_or_fusion.2), kind=kLoop, calls=%fused_computation.12.clone.1 | loop fusion | flops 10481664 | bytes 8683520 | tf_op jit(solution)/shard_map/while/body/eval_jaxpr/reduce_sum | solution.py:41
  74.5 1.2 copy-done.1
  75.8 2.3 fusion.86
  78.1 2.4 copy.196
  80.6 24.2 %dynamic_update_slice.19 = f32[2,512,2,4,80]{1,0,4,3,2:T(2,128)} dynamic-update-slice(f32[2,512,2,4,80]{1,0,4,3,2:T(2,128)} %get-tuple-element.375, f32[1,512,2,4,80]{1,0,4,3,2:T(1,128)} %copy.196, s32[]{:T(128)S(6)} %copy.204, s32[]{:T(128)} %constant.138.clone.1..sunk, s32[]{:T(128)} %constant.138.clone.1..sunk, s32[]{:T(128)} %constant.138.clone.1..sunk, s32[]{:T(128)} %constant.138.clone.1..sunk) | dynamic-update-slice | bytes 2621444 | tf_op jit(solution)/shard_map/while/body/jit(dynamic_update_index_in_dim)/dynamic_update_slice | solution.py:126
  106.9 1.2 and_or_fusion.2
  108.1 2.0 constant_dynamic-slice_fusion.3
  110.0 2.2 copy.193
  112.2 5.8 %bitcast_reduce_fusion.2 = (f32[512,2,4]{0,2,1:T(4,128)S(1)}, f32[2,512,4,512]{1,3,2,0:T(8,128)}) fusion(pred[512,512]{0,1:T(8,128)(4,1)S(1)} %and_or_fusion.2, bf16[512,2,4,80]{0,3,2,1:T(8,128)(2,1)} %bitcast.188, bf16[512,2,80]{0,2,1:T(8,128)(2,1)} %get-tuple-element.391), kind=kOutput, calls=%fused_computation.7.clone.1 | convolution fusion | flops 341831680 | bytes 9486336 | tf_op jit(solution)/shard_map/while/body/eval_jaxpr/nkgd,mkd->nkgm/dot_general | solution.py:34
  118.7 1.4 dynamic_update_slice.17
  120.1 4.6 %fusion.85 = f32[512,2,4]{0,2,1:T(4,128)S(1)} fusion(f32[2,512,4,512]{1,3,2,0:T(8,128)} %get-tuple-element.359, f32[512,2,4]{0,2,1:T(4,128)S(1)} %get-tuple-element.358, pred[512,512]{0,1:T(8,128)(4,1)S(1)} %and_or_fusion.2), kind=kLoop, calls=%fused_computation.12.clone.1 | loop fusion | flops 10481664 | bytes 8683520 | tf_op jit(solution)/shard_map/while/body/eval_jaxpr/reduce_sum | solution.py:41
  124.7 1.2 copy-done.1
  126.0 2.3 fusion.86
  128.3 2.4 copy.196
  130.8 24.2 %dynamic_update_slice.19 = f32[2,512,2,4,80]{1,0,4,3,2:T(2,128)} dynamic-update-slice(f32[2,512,2,4,80]{1,0,4,3,2:T(2,128)} %get-tuple-element.375, f32[1,512,2,4,80]{1,0,4,3,2:T(1,128)} %copy.196, s32[]{:T(128)S(6)} %copy.204, s32[]{:T(128)} %constant.138.clone.1..sunk, s32[]{:T(128)} %constant.138.clone.1..sunk, s32[]{:T(128)} %constant.138.clone.1..sunk, s32[]{:T(128)} %constant.138.clone.1..sunk) | dynamic-update-slice | bytes 2621444 | tf_op jit(solution)/shard_map/while/body/jit(dynamic_update_index_in_dim)/dynamic_update_slice | solution.py:126
  156.5 4.0 %all-to-all-start.1 = ((f32[8,128,2,4]{1,3,2,0:T(4,128)}), f32[8,128,2,4]{1,3,2,0:T(4,128)}, u32[]{:S(2)}, u32[]{:S(2)}) async-start(f32[8,128,2,4]{1,3,2,0:T(4,128)} %copy.135), calls=%async_computation.1 | async-start | bytes 65536 | tf_op jit(solution)/shard_map/all_to_all | solution.py:139
  161.1 1.0 copy.138
  162.1 1.8 gather_fusion
  165.4 4.1 %all-to-all-start.2 = ((f32[8,128,2,4]{1,3,2,0:T(4,128)}), f32[8,128,2,4]{1,3,2,0:T(4,128)S(1)}, u32[]{:S(2)}, u32[]{:S(2)}) async-start(f32[8,128,2,4]{1,3,2,0:T(4,128)} %copy.150), calls=%async_computation.2 | async-start | bytes 65536 | tf_op jit(solution)/shard_map/all_to_all | solution.py:140
  169.5 2.0 pad_maximum_fusion
  171.4 1.9 gather_fusion.1
  173.4 2.3 reshape.447
  175.7 3.7 reshape.446
  179.4 4.7 %reshape.442 = f32[8,128,2,4,80]{1,0,4,3,2:T(8,128)} reshape(f32[2,512,2,4,80]{1,0,4,3,2:T(2,128)} %get-tuple-element.70) | data formatting | bytes 5242880 | tf_op jit(solution)/shard_map/reshape | solution.py:136
  184.1 3.7 copy.133
  188.5 4.4 %all-to-all-start = ((f32[8,128,2,4,80]{1,4,3,2,0:T(8,128)}), f32[8,128,2,4,80]{1,4,3,2,0:T(8,128)}, u32[]{:S(2)}, u32[]{:S(2)}) async-start(f32[8,128,2,4,80]{1,4,3,2,0:T(8,128)} %copy.133), calls=%async_computation | async-start | bytes 5242880 | tf_op jit(solution)/shard_map/all_to_all | solution.py:141
  193.2 3.7 fusion.61
  196.9 1.4 fusion.65
  198.3 1.0 copy.160
  199.3 1.9 convolution_bitcast_fusion
  201.3 1.7 copy.146
  203.0 2.9 gather_fusion.3
  205.9 2.0 copy.148
  207.9 1.7 gather_fusion.2
  209.7 2.5 fusion.30
  212.2 1.1 copy.152
  213.3 1.4 gather_fusion.4
  214.7 1.0 copy.153
  217.3 7.9 %all-to-all-done = f32[8,128,2,4,80]{1,4,3,2,0:T(8,128)} async-done(((f32[8,128,2,4,80]{1,4,3,2,0:T(8,128)}), f32[8,128,2,4,80]{1,4,3,2,0:T(8,128)}, u32[]{:S(2)}, u32[]{:S(2)}) %all-to-all-start) | async-done | bytes 2621472 | tf_op jit(solution)/shard_map/all_to_all | solution.py:141
  225.2 2.1 multiply_reduce_fusion
  227.4 1.8 fusion.66
  229.5 59.2 %all-reduce.3.cloned.1.call-done = f32[128,2560]{1,0:T(8,128)} async-done(((f32[128,2560]{1,0:T(8,128)}), f32[128,2560]{1,0:T(8,128)}) %all-reduce.3.cloned.1.call-update) | async-done | bytes 1310736 | tf_op jit(solution)/shard_map/psum | solution.py:196
  288.7 1.8 fusion.24
  290.5 0.8 copy-done.3
  291.3 4.0 %fusion.45 = f32[128,896]{1,0:T(8,128)} fusion(bf16[2560,896]{1,0:T(8,128)(2,1)} %param.38, bf16[128,2560]{1,0:T(8,128)(2,1)S(1)} %get-tuple-element.228, f32[2560]{0:T(1024)S(1)} %convert_element_type.63, f32[128]{0:T(128)S(1)} %add_rsqrt_fusion.1), kind=kOutput, calls=%fused_computation.67 | convolution fusion | flops 588513280 | bytes 5712384 | tf_op jit(solution)/shard_map/dot_general | solution.py:199
  295.3 6.7 %fusion.29 = f32[128,2560]{1,0:T(8,128)} fusion(bf16[896,2560]{1,0:T(8,128)(2,1)} %param.40, bf16[2560,896]{1,0:T(8,128)(2,1)} %param.39, f32[128,896]{1,0:T(8,128)} %fusion.45, bf16[128,2560]{1,0:T(8,128)(2,1)} %copy-done.3, f32[2560]{0:T(1024)S(1)} %convert_element_type.63, f32[128]{0:T(128)S(1)} %add_rsqrt_fusion.1), kind=kOutput, calls=%fused_computation.50 | convolution fusion | flops 1176403968 | bytes 11610624 | tf_op jit(solution)/shard_map/dot_general | solution.py:202
  302.9 59.0 %all-reduce.5.cloned.1.call-done = f32[128,2560]{1,0:T(8,128)} async-done(((f32[128,2560]{1,0:T(8,128)}), f32[128,2560]{1,0:T(8,128)}) %all-reduce.5.cloned.1.call-update) | async-done | bytes 1310736 | tf_op jit(solution)/shard_map/psum | solution.py:202
  361.9 1.9 fusion.21
  363.8 2.7 convolution_convert_fusion.1
  366.6 1.4 convolution_convert_fusion
  (120 shorter events, 19.6 us)
Async XLA Ops:
  7.2 220.2 %copy-start = (bf16[640,2560]{1,0:T(8,128)(2,1)S(1)}, bf16[640,2560]{1,0:T(8,128)(2,1)}, u32[]{:S(2)}) copy-start(bf16[640,2560]{1,0:T(8,128)(2,1)} %param.36) | copy-start | bytes 9830404
  7.2 26.5 %copy-start.11 = (s32[4,128]{1,0:T(4,128)S(1)}, s32[4,128]{1,0:T(4,128)}, u32[]{:S(2)}) copy-start(s32[4,128]{1,0:T(4,128)} %constant.143.clone.1) | copy-start | bytes 6148
  7.2 12.8 %copy-start.14 = (s32[16]{0:T(128)S(1)}, s32[16]{0:T(128)}, u32[]{:S(2)}) copy-start(s32[16]{0:T(128)} %param.30) | copy-start | bytes 196
  7.2 13.4 %copy-start.19 = (s32[6]{0:T(128)S(1)}, s32[6]{0:T(128)}, u32[]{:S(2)}) copy-start(s32[6]{0:T(128)} %param.31) | copy-start | bytes 76
  7.2 13.5 %copy-start.15 = (s32[8]{0:T(128)S(1)}, s32[8]{0:T(128)}, u32[]{:S(2)}) copy-start(s32[8]{0:T(128)} %param.32) | copy-start | bytes 100
  7.2 25.0 %copy-start.5 = (s32[32]{0:T(128)S(1)}, s32[32]{0:T(128)}, u32[]{:S(2)}) copy-start(s32[32]{0:T(128)} %param.34) | copy-start | bytes 388
  7.2 30.9 %copy-start.20 = (s32[32]{0:T(128)S(1)}, s32[32]{0:T(128)}, u32[]{:S(2)}) copy-start(s32[32]{0:T(128)} %param.35) | copy-start | bytes 388
  7.2 47.4 %all-gather.2.cloned.1.call-start = ((), (), s32[]{:S(2)}) async-start(), calls=%async_computation.3 | async-start | bytes 1474560 | tf_op jit(solution)/shard_map/all_gather | solution.py:114
  15.7 5.0 %copy-start.21 = (s32[128]{0:T(128)}, s32[128]{0:T(128)S(1)}, u32[]{:S(2)}) copy-start(s32[128]{0:T(128)S(1)} %convert_reduce_fusion) | copy-start | bytes 1540
  69.9 5.8 %copy-start.1 = (f32[2,512,4,512]{1,3,2,0:T(8,128)S(1)}, f32[2,512,4,512]{1,3,2,0:T(8,128)}, u32[]{:S(2)}) copy-start(f32[2,512,4,512]{1,3,2,0:T(8,128)} %get-tuple-element.359) | copy-start | bytes 25165828 | tf_op jit(solution)/shard_map/while
  69.9 5.8 %copy-start.7 = (bf16[512,2,80]{0,2,1:T(8,128)(2,1)S(1)}, bf16[512,2,80]{0,2,1:T(8,128)(2,1)}, u32[]{:S(2)}) copy-start(bf16[512,2,80]{0,2,1:T(8,128)(2,1)} %get-tuple-element.392) | copy-start | bytes 491524 | tf_op jit(solution)/shard_map/while
  78.1 2.4 copy-start.9
  80.6 24.2 %copy-start.10 = (f32[2,512,2,4]{1,0,3,2:T(2,128)}, f32[2,512,2,4]{1,0,3,2:T(2,128)S(1)}, u32[]{:S(2)}) copy-start(f32[2,512,2,4]{1,0,3,2:T(2,128)S(1)} %dynamic_update_slice.18) | copy-start | bytes 98308 | tf_op jit(solution)/shard_map/while
  120.1 5.8 %copy-start.1 = (f32[2,512,4,512]{1,3,2,0:T(8,128)S(1)}, f32[2,512,4,512]{1,3,2,0:T(8,128)}, u32[]{:S(2)}) copy-start(f32[2,512,4,512]{1,3,2,0:T(8,128)} %get-tuple-element.359) | copy-start | bytes 25165828 | tf_op jit(solution)/shard_map/while
  120.1 5.8 %copy-start.7 = (bf16[512,2,80]{0,2,1:T(8,128)(2,1)S(1)}, bf16[512,2,80]{0,2,1:T(8,128)(2,1)}, u32[]{:S(2)}) copy-start(bf16[512,2,80]{0,2,1:T(8,128)(2,1)} %get-tuple-element.392) | copy-start | bytes 491524 | tf_op jit(solution)/shard_map/while
  128.3 2.4 copy-start.9
  130.8 24.2 %copy-start.10 = (f32[2,512,2,4]{1,0,3,2:T(2,128)}, f32[2,512,2,4]{1,0,3,2:T(2,128)S(1)}, u32[]{:S(2)}) copy-start(f32[2,512,2,4]{1,0,3,2:T(2,128)S(1)} %dynamic_update_slice.18) | copy-start | bytes 98308 | tf_op jit(solution)/shard_map/while
  155.1 16.4 %copy-start.2 = (bf16[128,640]{1,0:T(8,128)(2,1)S(1)}, bf16[128,640]{1,0:T(8,128)(2,1)}, u32[]{:S(2)}) copy-start(bf16[128,640]{1,0:T(8,128)(2,1)} %param.24) | copy-start | bytes 491524
  156.5 8.8 %all-to-all-start.1 = ((f32[8,128,2,4]{1,3,2,0:T(4,128)}), f32[8,128,2,4]{1,3,2,0:T(4,128)}, u32[]{:S(2)}, u32[]{:S(2)}) async-start(f32[8,128,2,4]{1,3,2,0:T(4,128)} %copy.135), calls=%async_computation.1 | async-start | bytes 65536 | tf_op jit(solution)/shard_map/all_to_all | solution.py:139
  165.4 22.5 %all-to-all-start.2 = ((f32[8,128,2,4]{1,3,2,0:T(4,128)}), f32[8,128,2,4]{1,3,2,0:T(4,128)S(1)}, u32[]{:S(2)}, u32[]{:S(2)}) async-start(f32[8,128,2,4]{1,3,2,0:T(4,128)} %copy.150), calls=%async_computation.2 | async-start | bytes 65536 | tf_op jit(solution)/shard_map/all_to_all | solution.py:140
  187.9 5.1 %copy-start.16 = (s32[16]{0:T(128)S(1)}, s32[16]{0:T(128)}, u32[]{:S(2)}) copy-start(s32[16]{0:T(128)} %param.28) | copy-start | bytes 196
  187.9 0.6 copy-start.8
  188.5 36.7 %all-to-all-start = ((f32[8,128,2,4,80]{1,4,3,2,0:T(8,128)}), f32[8,128,2,4,80]{1,4,3,2,0:T(8,128)}, u32[]{:S(2)}, u32[]{:S(2)}) async-start(f32[8,128,2,4,80]{1,4,3,2,0:T(8,128)} %copy.133), calls=%async_computation | async-start | bytes 5242880 | tf_op jit(solution)/shard_map/all_to_all | solution.py:141
  192.9 95.8 %all-reduce.3.cloned.1.call-start = ((), (), s32[]{:S(2)}) async-start(), calls=%async_computation.4 | async-start | bytes 2621440 | tf_op jit(solution)/shard_map/psum | solution.py:196
  193.0 4.0 %copy-start.6 = (bf16[16,16,2,4,80]{4,3,2,1,0:T(4,128)(2,1)S(1)}, bf16[16,16,2,4,80]{4,3,2,1,0:T(4,128)(2,1)}, u32[]{:S(2)}) copy-start(bf16[16,16,2,4,80]{4,3,2,1,0:T(4,128)(2,1)} %reshape.447) | copy-start | bytes 983044
  201.2 1.8 copy-start.17
  201.2 1.8 copy-start.22
  225.2 2.1 copy-start.4
  227.3 2.1 copy-start.12
  229.2 132.7 %all-reduce.5.cloned.1.call-start = ((), (), s32[]{:S(2)}) async-start(), calls=%async_computation.5 | async-start | bytes 2621440 | tf_op jit(solution)/shard_map/psum | solution.py:202
  290.5 0.9 copy-start.3
  295.3 6.8 %copy-start.13 = (bf16[2560]{0:T(1024)(128)(2,1)S(1)}, bf16[2560]{0:T(1024)(128)(2,1)}, u32[]{:S(2)}) copy-start(bf16[2560]{0:T(1024)(128)(2,1)} %param.41) | copy-start | bytes 15364
  361.9 4.7 %copy-start.18 = (bf16[2560,640]{1,0:T(8,128)(2,1)S(1)}, bf16[2560,640]{1,0:T(8,128)(2,1)}, u32[]{:S(2)}) copy-start(bf16[2560,640]{1,0:T(8,128)(2,1)} %param.42) | copy-start | bytes 9830404
Sparse Core Ops, SparseCore 0:
  10.0 27.2 all-gather.1
  229.3 59.3 all-reduce.2
  302.2 59.6 all-reduce.4
where the time goes:
time: 381 us; the launch traced here: 375 us
  waiting for transfers between devices  127 us (33%)
  local copies, waits for them, and re-layouts  125 us (33%)
  other arithmetic  49 us (13%)
  matrix products  36.3 us (10%)
  between operations  14.1 us (4%)
  starting transfers between devices  12.8 us (3%)
  blocking collectives  11.4 us (3%)
    psum x1, waiting for transfers between devices, per_device(): lax.psum(jnp.dot(attention, out_weight, preferred_element_type=jnp.float3...  59.2 us
    psum x1, waiting for transfers between devices, per_device(): lax.psum(jnp.dot(hidden, down_weight, preferred_element_type=jnp.float32)...  59 us
    dynamic_update_slice x12, local copies, waits for them, and re-layouts, visit_owners(): lax.map(owner_block, (all_query.reshape(total_rows // block, block, all_q...  57.6 us
    select_n x1, other arithmetic, pool_split(): jnp.repeat(node_of_page, page_size, total_repeat_length=page_count * page...  16 us
    dot_general x3, matrix products, attend(): jnp.einsum('nkgd,mkd->nkgm', queries, keys, preferred_element_type=jnp.fl...  13.1 us
    reduce_sum x3, other arithmetic, attend(): total = jnp.sum(raised, axis=-1)  11.8 us
    all_gather x1, blocking collectives, visit_owners(): lax.all_gather(token_info, 'req', axis=0, tiled=True)  11.4 us
    reshape x6, local copies, waits for them, and re-layouts, visit_owners(): item.reshape((holders, row_count) + item.shape[2:])  11.4 us
  transfers between devices with their start and end apart: 6, of which 3 were waited for; matrix products, arithmetic and copies ran while one was open for 22% of the time, Pallas kernels for 0%

commit v1 on v0

--- a/solution.py
+++ b/solution.py
@@ -112,7 +112,9 @@
 def visit_owners(new_query, token_info, prefix_pool, page_node, page_rank, kv_local, group):
     all_query, all_info = (
         lax.all_gather(new_query, "req", axis=0, tiled=True),
-        lax.all_gather(token_info, "req", axis=0, tiled=True),
+        jnp.concatenate(
+            lax.all_to_all(jnp.stack([token_info] * lax.axis_size("req")), "req", 0, 0), axis=0
+        ),
     )
     total_rows = all_query.shape[0]
     block = math.gcd(total_rows, 512)

time: 381 us -> 382 us (level)
  blocking collectives: 11.4 us -> 0 us
  starting transfers between devices: 12.8 us -> 18.3 us
    all_gather x1 -> x0, blocking collectives: 11.4 us -> none  [visit_owners(): lax.all_gather(token_info, 'req', axis=0, tiled=True)]
    all_to_all x0 -> x1, starting transfers between devices: none -> 5.17 us  [visit_owners(): lax.all_to_all(jnp.stack([token_info] * lax.axis_size('req')), 'req', 0, 0)]
  transfers between devices with their start and end apart: 6 -> 7, of which waited for: 3 -> 4; matrix products, arithmetic and copies ran while one was open for 22% -> 24% of each run, Pallas kernels for 0% -> 0%
where the time goes in v1:
time: 382 us; the launch traced here: 377 us
  local copies, waits for them, and re-layouts  128 us (34%)
  waiting for transfers between devices  127 us (33%)
  other arithmetic  52.7 us (14%)
  matrix products  36.3 us (10%)
  starting transfers between devices  18.3 us (5%)
  between operations  14 us (4%)
    psum x1, waiting for transfers between devices, per_device(): lax.psum(jnp.dot(attention, out_weight, preferred_element_type=jnp.float3...  59.4 us
    psum x1, waiting for transfers between devices, per_device(): lax.psum(jnp.dot(hidden, down_weight, preferred_element_type=jnp.float32)...  59 us
    dynamic_update_slice x12, local copies, waits for them, and re-layouts, visit_owners(): lax.map(owner_block, (all_query.reshape(total_rows // block, block, all_q...  57.6 us
    select_n x1, other arithmetic, pool_split(): jnp.repeat(node_of_page, page_size, total_repeat_length=page_count * page...  16.7 us
    dot_general x3, matrix products, attend(): jnp.einsum('nkgd,mkd->nkgm', queries, keys, preferred_element_type=jnp.fl...  13.1 us
    reduce_sum x3, other arithmetic, attend(): total = jnp.sum(raised, axis=-1)  11.8 us
    reshape x6, local copies, waits for them, and re-layouts, visit_owners(): item.reshape((holders, row_count) + item.shape[2:])  11.4 us
    gather x6, local copies, waits for them, and re-layouts, local_part(): item.reshape((requests * MAXNEW,) + item.shape[2:])[flat]  8.97 us
  transfers between devices with their start and end apart: 7, of which 4 were waited for; matrix products, arithmetic and copies ran while one was open for 24% of the time, Pallas kernels for 0%

profile of v1, /device:TPU:0, one launch (start us, length us, event | category | flops | bytes accessed | tf_op | source)
XLA Modules:
  0.0 376.6 jit_solution(4011879178154455613)
XLA Ops:
  10.2 1.2 select_reduce_fusion.1
  13.6 5.2 %all-to-all-start = ((s32[8,128,4]{1,2,0:T(4,128)}), s32[8,128,4]{1,2,0:T(4,128)}, u32[]{:S(2)}, u32[]{:S(2)}) async-start(s32[8,128,4]{1,2,0:T(4,128)} %stack.28), calls=%async_computation | async-start | bytes 32768 | tf_op jit(solution)/shard_map/all_to_all | solution.py:116
  18.8 2.1 reshape.439
  20.9 1.8 fusion.64
  22.7 2.1 fusion.63
  25.5 4.3 %compare_select_fusion.2 = (s32[512,1]{0,1:T(1,128)S(1)}, s32[512,1]{0,1:T(1,128)S(1)}) fusion(s32[]{:T(128)} %bitcast.29, s32[]{:T(128)} %bitcast.30, s32[]{:T(128)} %bitcast.31, s32[]{:T(128)} %bitcast.32, s32[]{:T(128)} %bitcast.33, s32[]{:T(128)} %bitcast.35, s32[]{:T(128)} %bitcast.34, s32[512,1]{0,1:T(1,128)S(1)} %bitcast.213, s32[512,1]{0,1:T(1,128)S(1)} %bitcast.212), kind=kLoop, calls=%fused_computation.105 | loop fusion | flops 7168 | bytes 8220 | tf_op jit(solution)/shard_map/jit(_take)/gather | solution.py:52
  30.7 16.7 %select_select_fusion = s32[512]{0:T(512)} fusion(pred[512]{0:T(512)(128)(4,1)S(1)} %get-tuple-element.190, pred[512]{0:T(512)(128)(4,1)S(1)} %get-tuple-element.189, pred[512]{0:T(512)(128)(4,1)S(1)} %get-tuple-element.188, pred[512]{0:T(512)(128)(4,1)S(1)} %get-tuple-element.187, pred[512]{0:T(512)(128)(4,1)S(1)} %get-tuple-element.186, ...), kind=kLoop, calls=%fused_computation.129 | loop fusion | flops 17408 | bytes 19060 | tf_op jit(solution)/shard_map/jit(_take)/select_n | solution.py:52
  47.4 3.1 fusion.62
  51.7 1.8 copy.132
  53.6 1.8 copy.131
  55.4 100.6 %while.16 = (s32[]{:T(128)}, f32[2,512,2,4]{1,0,3,2:T(2,128)}, f32[2,512,2,4]{1,0,3,2:T(2,128)}, f32[2,512,2,4,80]{1,0,4,3,2:T(2,128)}, s32[512]{0:T(512)}, /*in...) while((s32[]{:T(128)}, f32[2,512,2,4]{1,0,3,2:T(2,128)}, ...), condition=%wide.region_9.10_spmd.clone, body=%wide.region_6.0_spmd.clone.sunk | while | flops 700178944 | bytes 71092600 | solution.py:128
  57.5 1.2 and_or_fusion.2
  58.7 2.0 constant_dynamic-slice_fusion.3
  60.7 2.2 copy.196
  62.9 5.8 %bitcast_reduce_fusion.2 = (f32[512,2,4]{0,2,1:T(4,128)S(1)}, f32[2,512,4,512]{1,3,2,0:T(8,128)}) fusion(pred[512,512]{0,1:T(8,128)(4,1)S(1)} %and_or_fusion.2, bf16[512,2,4,80]{0,3,2,1:T(8,128)(2,1)} %bitcast.188, bf16[512,2,80]{0,2,1:T(8,128)(2,1)} %get-tuple-element.381), kind=kOutput, calls=%fused_computation.7.clone.1 | convolution fusion | flops 341831680 | bytes 9486336 | tf_op jit(solution)/shard_map/while/body/eval_jaxpr/nkgd,mkd->nkgm/dot_general | solution.py:34
  69.3 1.4 dynamic_update_slice.17
  70.8 4.6 %fusion.85 = f32[512,2,4]{0,2,1:T(4,128)S(1)} fusion(f32[2,512,4,512]{1,3,2,0:T(8,128)} %get-tuple-element.349, f32[512,2,4]{0,2,1:T(4,128)S(1)} %get-tuple-element.348, pred[512,512]{0,1:T(8,128)(4,1)S(1)} %and_or_fusion.2), kind=kLoop, calls=%fused_computation.12.clone.1 | loop fusion | flops 10481664 | bytes 8683520 | tf_op jit(solution)/shard_map/while/body/eval_jaxpr/reduce_sum | solution.py:41
  75.4 1.2 copy-done.1
  76.6 2.3 fusion.86
  78.9 2.4 copy.199
  81.5 24.2 %dynamic_update_slice.19 = f32[2,512,2,4,80]{1,0,4,3,2:T(2,128)} dynamic-update-slice(f32[2,512,2,4,80]{1,0,4,3,2:T(2,128)} %get-tuple-element.365, f32[1,512,2,4,80]{1,0,4,3,2:T(1,128)} %copy.199, s32[]{:T(128)S(6)} %copy.207, s32[]{:T(128)} %constant.138.clone.1..sunk, s32[]{:T(128)} %constant.138.clone.1..sunk, s32[]{:T(128)} %constant.138.clone.1..sunk, s32[]{:T(128)} %constant.138.clone.1..sunk) | dynamic-update-slice | bytes 2621444 | tf_op jit(solution)/shard_map/while/body/jit(dynamic_update_index_in_dim)/dynamic_update_slice | solution.py:128
  107.8 1.2 and_or_fusion.2
  109.0 2.0 constant_dynamic-slice_fusion.3
  111.0 2.2 copy.196
  113.2 5.8 %bitcast_reduce_fusion.2 = (f32[512,2,4]{0,2,1:T(4,128)S(1)}, f32[2,512,4,512]{1,3,2,0:T(8,128)}) fusion(pred[512,512]{0,1:T(8,128)(4,1)S(1)} %and_or_fusion.2, bf16[512,2,4,80]{0,3,2,1:T(8,128)(2,1)} %bitcast.188, bf16[512,2,80]{0,2,1:T(8,128)(2,1)} %get-tuple-element.381), kind=kOutput, calls=%fused_computation.7.clone.1 | convolution fusion | flops 341831680 | bytes 9486336 | tf_op jit(solution)/shard_map/while/body/eval_jaxpr/nkgd,mkd->nkgm/dot_general | solution.py:34
  119.6 1.4 dynamic_update_slice.17
  121.0 4.6 %fusion.85 = f32[512,2,4]{0,2,1:T(4,128)S(1)} fusion(f32[2,512,4,512]{1,3,2,0:T(8,128)} %get-tuple-element.349, f32[512,2,4]{0,2,1:T(4,128)S(1)} %get-tuple-element.348, pred[512,512]{0,1:T(8,128)(4,1)S(1)} %and_or_fusion.2), kind=kLoop, calls=%fused_computation.12.clone.1 | loop fusion | flops 10481664 | bytes 8683520 | tf_op jit(solution)/shard_map/while/body/eval_jaxpr/reduce_sum | solution.py:41
  125.7 1.2 copy-done.1
  126.9 2.3 fusion.86
  129.2 2.4 copy.199
  131.8 24.2 %dynamic_update_slice.19 = f32[2,512,2,4,80]{1,0,4,3,2:T(2,128)} dynamic-update-slice(f32[2,512,2,4,80]{1,0,4,3,2:T(2,128)} %get-tuple-element.365, f32[1,512,2,4,80]{1,0,4,3,2:T(1,128)} %copy.199, s32[]{:T(128)S(6)} %copy.207, s32[]{:T(128)} %constant.138.clone.1..sunk, s32[]{:T(128)} %constant.138.clone.1..sunk, s32[]{:T(128)} %constant.138.clone.1..sunk, s32[]{:T(128)} %constant.138.clone.1..sunk) | dynamic-update-slice | bytes 2621444 | tf_op jit(solution)/shard_map/while/body/jit(dynamic_update_index_in_dim)/dynamic_update_slice | solution.py:128
  157.4 4.2 %all-to-all-start.2 = ((f32[8,128,2,4]{1,3,2,0:T(4,128)}), f32[8,128,2,4]{1,3,2,0:T(4,128)}, u32[]{:S(2)}, u32[]{:S(2)}) async-start(f32[8,128,2,4]{1,3,2,0:T(4,128)} %copy.138), calls=%async_computation.2 | async-start | bytes 65536 | tf_op jit(solution)/shard_map/all_to_all | solution.py:141
  162.3 1.0 copy.141
  163.3 1.8 gather_fusion
  166.6 4.1 %all-to-all-start.3 = ((f32[8,128,2,4]{1,3,2,0:T(4,128)}), f32[8,128,2,4]{1,3,2,0:T(4,128)S(1)}, u32[]{:S(2)}, u32[]{:S(2)}) async-start(f32[8,128,2,4]{1,3,2,0:T(4,128)} %copy.153), calls=%async_computation.3 | async-start | bytes 65536 | tf_op jit(solution)/shard_map/all_to_all | solution.py:142
  170.7 2.0 pad_maximum_fusion
  172.7 1.9 gather_fusion.1
  174.6 2.3 reshape.445
  177.0 3.7 reshape.444
  180.7 4.7 %reshape.440 = f32[8,128,2,4,80]{1,0,4,3,2:T(8,128)} reshape(f32[2,512,2,4,80]{1,0,4,3,2:T(2,128)} %get-tuple-element.70) | data formatting | bytes 5242880 | tf_op jit(solution)/shard_map/reshape | solution.py:138
  185.4 3.7 copy.136
  189.8 4.4 %all-to-all-start.1 = ((f32[8,128,2,4,80]{1,4,3,2,0:T(8,128)}), f32[8,128,2,4,80]{1,4,3,2,0:T(8,128)}, u32[]{:S(2)}, u32[]{:S(2)}) async-start(f32[8,128,2,4,80]{1,4,3,2,0:T(8,128)} %copy.136), calls=%async_computation.1 | async-start | bytes 5242880 | tf_op jit(solution)/shard_map/all_to_all | solution.py:143
  194.5 3.7 fusion.61
  198.2 1.4 fusion.65
  200.6 1.9 convolution_bitcast_fusion
  202.6 1.7 copy.149
  204.3 2.9 gather_fusion.3
  207.2 2.0 copy.151
  209.1 1.7 gather_fusion.2
  210.9 2.5 fusion.30
  213.5 1.1 copy.155
  214.6 1.4 gather_fusion.4
  216.0 1.0 copy.156
  218.6 7.9 %all-to-all-done.1 = f32[8,128,2,4,80]{1,4,3,2,0:T(8,128)} async-done(((f32[8,128,2,4,80]{1,4,3,2,0:T(8,128)}), f32[8,128,2,4,80]{1,4,3,2,0:T(8,128)}, u32[]{:S(2)}, u32[]{:S(2)}) %all-to-all-start.1) | async-done | bytes 2621472 | tf_op jit(solution)/shard_map/all_to_all | solution.py:143
  226.5 2.1 multiply_reduce_fusion
  228.6 1.8 fusion.66
  230.7 59.4 %all-reduce.3.cloned.1.call-done = f32[128,2560]{1,0:T(8,128)} async-done(((f32[128,2560]{1,0:T(8,128)}), f32[128,2560]{1,0:T(8,128)}) %all-reduce.3.cloned.1.call-update) | async-done | bytes 1310736 | tf_op jit(solution)/shard_map/psum | solution.py:198
  290.1 1.8 fusion.24
  292.7 4.0 %fusion.45 = f32[128,896]{1,0:T(8,128)} fusion(bf16[2560,896]{1,0:T(8,128)(2,1)} %param.38, bf16[128,2560]{1,0:T(8,128)(2,1)S(1)} %get-tuple-element.218, f32[2560]{0:T(1024)S(1)} %convert_element_type.63, f32[128]{0:T(128)S(1)} %add_rsqrt_fusion.1), kind=kOutput, calls=%fused_computation.67 | convolution fusion | flops 588513280 | bytes 5712384 | tf_op jit(solution)/shard_map/dot_general | solution.py:201
  296.7 6.7 %fusion.29 = f32[128,2560]{1,0:T(8,128)} fusion(bf16[896,2560]{1,0:T(8,128)(2,1)} %param.40, bf16[2560,896]{1,0:T(8,128)(2,1)} %param.39, f32[128,896]{1,0:T(8,128)} %fusion.45, bf16[128,2560]{1,0:T(8,128)(2,1)} %copy-done.3, f32[2560]{0:T(1024)S(1)} %convert_element_type.63, f32[128]{0:T(128)S(1)} %add_rsqrt_fusion.1), kind=kOutput, calls=%fused_computation.50 | convolution fusion | flops 1176403968 | bytes 11610624 | tf_op jit(solution)/shard_map/dot_general | solution.py:204
  304.3 59.0 %all-reduce.5.cloned.1.call-done = f32[128,2560]{1,0:T(8,128)} async-done(((f32[128,2560]{1,0:T(8,128)}), f32[128,2560]{1,0:T(8,128)}) %all-reduce.5.cloned.1.call-update) | async-done | bytes 1310736 | tf_op jit(solution)/shard_map/psum | solution.py:204
  363.3 1.9 fusion.21
  365.3 2.7 convolution_convert_fusion.1
  368.0 1.4 convolution_convert_fusion
  (112 shorter events, 23.6 us)
Async XLA Ops:
  7.2 221.4 %copy-start = (bf16[640,2560]{1,0:T(8,128)(2,1)S(1)}, bf16[640,2560]{1,0:T(8,128)(2,1)}, u32[]{:S(2)}) copy-start(bf16[640,2560]{1,0:T(8,128)(2,1)} %param.36) | copy-start | bytes 9830404
  7.2 43.3 %copy-start.15 = (s32[32]{0:T(128)S(1)}, s32[32]{0:T(128)}, u32[]{:S(2)}) copy-start(s32[32]{0:T(128)} %param.35) | copy-start | bytes 388
  7.2 48.2 %all-gather.2.cloned.1.call-start = ((), (), s32[]{:S(2)}) async-start(), calls=%async_computation.4 | async-start | bytes 1474560 | tf_op jit(solution)/shard_map/all_gather | solution.py:114
  9.7 0.5 copy-start.16
  13.6 41.8 %all-to-all-start = ((s32[8,128,4]{1,2,0:T(4,128)}), s32[8,128,4]{1,2,0:T(4,128)}, u32[]{:S(2)}, u32[]{:S(2)}) async-start(s32[8,128,4]{1,2,0:T(4,128)} %stack.28), calls=%async_computation | async-start | bytes 32768 | tf_op jit(solution)/shard_map/all_to_all | solution.py:116
  70.8 5.8 %copy-start.1 = (f32[2,512,4,512]{1,3,2,0:T(8,128)S(1)}, f32[2,512,4,512]{1,3,2,0:T(8,128)}, u32[]{:S(2)}) copy-start(f32[2,512,4,512]{1,3,2,0:T(8,128)} %get-tuple-element.349) | copy-start | bytes 25165828 | tf_op jit(solution)/shard_map/while
  70.8 5.8 %copy-start.6 = (bf16[512,2,80]{0,2,1:T(8,128)(2,1)S(1)}, bf16[512,2,80]{0,2,1:T(8,128)(2,1)}, u32[]{:S(2)}) copy-start(bf16[512,2,80]{0,2,1:T(8,128)(2,1)} %get-tuple-element.382) | copy-start | bytes 491524 | tf_op jit(solution)/shard_map/while
  78.9 2.4 copy-start.8
  81.5 24.2 %copy-start.9 = (f32[2,512,2,4]{1,0,3,2:T(2,128)}, f32[2,512,2,4]{1,0,3,2:T(2,128)S(1)}, u32[]{:S(2)}) copy-start(f32[2,512,2,4]{1,0,3,2:T(2,128)S(1)} %dynamic_update_slice.18) | copy-start | bytes 98308 | tf_op jit(solution)/shard_map/while
  121.0 5.8 %copy-start.1 = (f32[2,512,4,512]{1,3,2,0:T(8,128)S(1)}, f32[2,512,4,512]{1,3,2,0:T(8,128)}, u32[]{:S(2)}) copy-start(f32[2,512,4,512]{1,3,2,0:T(8,128)} %get-tuple-element.349) | copy-start | bytes 25165828 | tf_op jit(solution)/shard_map/while
  121.0 5.8 %copy-start.6 = (bf16[512,2,80]{0,2,1:T(8,128)(2,1)S(1)}, bf16[512,2,80]{0,2,1:T(8,128)(2,1)}, u32[]{:S(2)}) copy-start(bf16[512,2,80]{0,2,1:T(8,128)(2,1)} %get-tuple-element.382) | copy-start | bytes 491524 | tf_op jit(solution)/shard_map/while
  129.2 2.4 copy-start.8
  131.8 24.2 %copy-start.9 = (f32[2,512,2,4]{1,0,3,2:T(2,128)}, f32[2,512,2,4]{1,0,3,2:T(2,128)S(1)}, u32[]{:S(2)}) copy-start(f32[2,512,2,4]{1,0,3,2:T(2,128)S(1)} %dynamic_update_slice.18) | copy-start | bytes 98308 | tf_op jit(solution)/shard_map/while
  156.0 16.7 %copy-start.2 = (bf16[128,640]{1,0:T(8,128)(2,1)S(1)}, bf16[128,640]{1,0:T(8,128)(2,1)}, u32[]{:S(2)}) copy-start(bf16[128,640]{1,0:T(8,128)(2,1)} %param.24) | copy-start | bytes 491524
  157.4 9.2 %all-to-all-start.2 = ((f32[8,128,2,4]{1,3,2,0:T(4,128)}), f32[8,128,2,4]{1,3,2,0:T(4,128)}, u32[]{:S(2)}, u32[]{:S(2)}) async-start(f32[8,128,2,4]{1,3,2,0:T(4,128)} %copy.138), calls=%async_computation.2 | async-start | bytes 65536 | tf_op jit(solution)/shard_map/all_to_all | solution.py:141
  166.6 22.6 %all-to-all-start.3 = ((f32[8,128,2,4]{1,3,2,0:T(4,128)}), f32[8,128,2,4]{1,3,2,0:T(4,128)S(1)}, u32[]{:S(2)}, u32[]{:S(2)}) async-start(f32[8,128,2,4]{1,3,2,0:T(4,128)} %copy.153), calls=%async_computation.3 | async-start | bytes 65536 | tf_op jit(solution)/shard_map/all_to_all | solution.py:142
  189.2 5.1 %copy-start.12 = (s32[16]{0:T(128)S(1)}, s32[16]{0:T(128)}, u32[]{:S(2)}) copy-start(s32[16]{0:T(128)} %param.28) | copy-start | bytes 196
  189.2 0.6 copy-start.7
  189.8 36.7 %all-to-all-start.1 = ((f32[8,128,2,4,80]{1,4,3,2,0:T(8,128)}), f32[8,128,2,4,80]{1,4,3,2,0:T(8,128)}, u32[]{:S(2)}, u32[]{:S(2)}) async-start(f32[8,128,2,4,80]{1,4,3,2,0:T(8,128)} %copy.136), calls=%async_computation.1 | async-start | bytes 5242880 | tf_op jit(solution)/shard_map/all_to_all | solution.py:143
  194.2 96.0 %all-reduce.3.cloned.1.call-start = ((), (), s32[]{:S(2)}) async-start(), calls=%async_computation.5 | async-start | bytes 2621440 | tf_op jit(solution)/shard_map/psum | solution.py:198
  194.2 4.0 %copy-start.5 = (bf16[16,16,2,4,80]{4,3,2,1,0:T(4,128)(2,1)S(1)}, bf16[16,16,2,4,80]{4,3,2,1,0:T(4,128)(2,1)}, u32[]{:S(2)}) copy-start(bf16[16,16,2,4,80]{4,3,2,1,0:T(4,128)(2,1)} %reshape.445) | copy-start | bytes 983044
  202.5 1.8 copy-start.13
  202.5 1.8 copy-start.17
  226.5 2.1 copy-start.4
  228.6 2.1 copy-start.10
  230.4 132.9 %all-reduce.5.cloned.1.call-start = ((), (), s32[]{:S(2)}) async-start(), calls=%async_computation.6 | async-start | bytes 2621440 | tf_op jit(solution)/shard_map/psum | solution.py:204
  291.9 0.9 copy-start.3
  296.7 6.8 %copy-start.11 = (bf16[2560]{0:T(1024)(128)(2,1)S(1)}, bf16[2560]{0:T(1024)(128)(2,1)}, u32[]{:S(2)}) copy-start(bf16[2560]{0:T(1024)(128)(2,1)} %param.41) | copy-start | bytes 15364
  363.3 4.7 %copy-start.14 = (bf16[2560,640]{1,0:T(8,128)(2,1)S(1)}, bf16[2560,640]{1,0:T(8,128)(2,1)}, u32[]{:S(2)}) copy-start(bf16[2560,640]{1,0:T(8,128)(2,1)} %param.42) | copy-start | bytes 9830404
Sparse Core Ops, SparseCore 0:
  9.9 27.3 all-gather.1
  230.6 59.5 all-reduce.2
  303.6 59.6 all-reduce.4
